TPU v7x, 256 devices: a whole 4x4x8 slice. The times are simulated.
256 devices in a mesh: section: 16 (over z, core), mp: 8 (over x, y_hi), dp: 2 (over y_lo).
Axes of the slice: x: 4, y: 4 (y_hi: 2, y_lo: 2; y = y_hi * 2 + y_lo), z: 8, core: 2. Of those that a mesh axis runs over, the one named last changes fastest.
Arguments:
- enc_out: bfloat16 [2, 512, 4096], P('dp', 'mp', 'section'), may hold values from -6 to 6
- kv_weight: bfloat16 [16, 4096, 2, 4096], P('section', None, None, 'mp'), may hold values from -0.09375 to 0.09375
- dec_query: bfloat16 [16, 2, 512, 4096], P('section', 'dp', None, 'mp'), may hold values from -120 to 120
- ctx_grad: bfloat16 [16, 2, 512, 4096], P('section', 'dp', None, 'mp'), may hold values from -6 to 6
- enc_seg: int32 [2, 512], P('dp'), may hold values from 0 to 7, never falling along the last dimension, each value on 1 to 128 neighbouring positions
- dec_seg: int32 [2, 512], P('dp'), may hold values from 0 to 7, never falling along the last dimension, each value on 1 to 128 neighbouring positions
Outputs:
- context: bfloat16 [16, 2, 512, 4096], P('section', 'dp', None, 'mp')
- enc_grad: float32 [2, 512, 4096], P('dp', 'mp', 'section')
Inputs may be any that keep to these rules, and one draw needn't show every extreme that they name: `enc_seg`: document ids never fall along a sequence and every id appears. `dec_seg`: document ids never fall along a sequence and every id appears.
All inputs are finite; a program needn't handle non-finite values.
Results may differ from a plain program's by a relative error of at most 0.04.
The roundings to bfloat16 on the way count: a program that leaves them out, or rounds other values in their place, can miss the bound.
Values may be sent and summed in bfloat16 or wider, within the bound.
No kernel may reach another device: no remote copies, remote signals or barrier semaphores. Data moves between devices by JAX's collectives and lax.ppermute only.
A program may use at most 128 MiB of HBM per device.

v0:
```python
import jax
import jax.numpy as jnp
from jax import lax
from jax.sharding import PartitionSpec as P

HD = 256


def attend(query, keys, values, grad, same_doc):
    scale = HD ** (-0.5)
    scores = jnp.einsum("qhd,khd->hqk", query, keys, preferred_element_type=jnp.float32) * scale
    scores = jnp.where(same_doc[None], scores, -1e30)
    top_score = jnp.max(scores, axis=-1, keepdims=True)
    raised = jnp.exp(scores - top_score)
    probs = raised / jnp.sum(raised, axis=-1, keepdims=True)
    probs_low = probs.astype(jnp.bfloat16)
    context = jnp.einsum(
        "hqk,khd->qhd", probs_low, values, preferred_element_type=jnp.float32
    ).astype(jnp.bfloat16)
    grad_values = jnp.einsum(
        "hqk,qhd->khd", probs_low, grad, preferred_element_type=jnp.float32
    ).astype(jnp.bfloat16)
    grad_probs = jnp.einsum("qhd,khd->hqk", grad, values, preferred_element_type=jnp.float32)
    inner_sum = jnp.sum(probs * grad_probs, axis=-1, keepdims=True)
    grad_scores = (probs * (grad_probs - inner_sum) * scale).astype(jnp.bfloat16)
    grad_keys = jnp.einsum(
        "hqk,qhd->khd", grad_scores, query, preferred_element_type=jnp.float32
    ).astype(jnp.bfloat16)
    return (context, grad_keys, grad_values)


def per_device(enc_out, kv_weight, dec_query, ctx_grad, enc_seg, dec_seg):
    shard_rows = enc_out[0]
    width = kv_weight.shape[3]
    model_width = kv_weight.shape[1]
    flat_weight = kv_weight[0].reshape(model_width, 2 * width)
    all_tokens = lax.all_gather(shard_rows, "mp", axis=0, tiled=True)
    weight_rows = flat_weight
    key_values = jnp.dot(
        lax.all_gather(all_tokens, "section", axis=1, tiled=True),
        weight_rows,
        preferred_element_type=jnp.float32,
    ).astype(jnp.bfloat16)
    length = key_values.shape[0]
    heads_here = width // HD
    decoder = dec_query.shape[2]
    keys = key_values[:, :width].reshape(length, heads_here, HD)
    values = key_values[:, width:].reshape(length, heads_here, HD)
    same_doc = dec_seg[0][:, None] == enc_seg[0][None, :]
    query = dec_query[0, 0].reshape(decoder, heads_here, HD)
    grad = ctx_grad[0, 0].reshape(decoder, heads_here, HD)
    context, grad_keys, grad_values = attend(query, keys, values, grad, same_doc)
    grad_both = jnp.concatenate(
        [grad_keys.reshape(length, width), grad_values.reshape(length, width)], axis=1
    )
    weight_rows = flat_weight
    feature_share = lax.psum_scatter(
        lax.dot_general(
            weight_rows, grad_both, (((1,), (1,)), ((), ())), preferred_element_type=jnp.float32
        ).astype(jnp.bfloat16),
        "section",
        scatter_dimension=0,
        tiled=True,
    )
    owned_grad = (
        lax.psum_scatter(feature_share, "mp", scatter_dimension=1, tiled=True).astype(jnp.float32).T
    )
    return (context.reshape(1, 1, decoder, width), owned_grad[None])


def solution(mesh):
    placed = (
        P("dp", "mp", "section"),
        P("section", None, None, "mp"),
        P("section", "dp", None, "mp"),
        P("section", "dp", None, "mp"),
        P("dp", None),
        P("dp", None),
    )
    return jax.shard_map(
        per_device,
        mesh=mesh,
        in_specs=placed,
        out_specs=(P("section", "dp", None, "mp"), P("dp", "mp", "section")),
        check_vma=False,
    )
```

profile of v0, /device:TPU:1, one launch (start us, length us, event | category | flops | bytes accessed | tf_op | source)
XLA Modules:
  0.0 273.2 jit_solution(1828879622895667745)
XLA Ops:
  7.2 0.0 all-gather.4.cloned.1.call-start
  7.2 31.4 %all-gather = bf16[1,512,256]{2,1,0:T(8,128)(2,1)} all-gather(bf16[1,64,256]{2,1,0:T(8,128)(2,1)} %param.6), channel_id=2, replica_groups=mesh['section'=16,'mp'=8,'dp'=2] {'mp'}, dimensions={1}, use_global_device_ids=true | all-gather | bytes 294912 | tf_op jit(solution)/shard_map/all_gather | solution.py:37
  38.6 0.0 all-gather.4.cloned.1.call-update
  38.6 0.0 reduce-scatter.3.cloned.1.call-start
  38.7 2.1 copy.23
  40.7 1.3 copy.24
  42.0 9.5 %copy.27 = bf16[512,8,2,512]{3,1,2,0:T(8,128)(2,1)} copy(bf16[512,8,2,512]{3,2,1,0:T(2,128)(2,1)} %bitcast.75) | data formatting | bytes 16777216
  51.5 0.2 broadcast_compare_fusion
  51.7 45.6 %all-gather.4.cloned.1.call-done = bf16[1,512,4096]{2,1,0:T(8,128)(2,1)} async-done(((bf16[1,512,256]{2,1,0:T(8,128)(2,1)}), bf16[1,512,4096]{2,1,0:T(8,128)(2,1)}) %all-gather.4.cloned.1.call-update) | async-done | bytes 4194320 | tf_op jit(solution)/shard_map/all_gather | solution.py:40
  97.3 9.1 %fusion.10 = bf16[512,1024]{1,0:T(8,128)(2,1)S(1)} fusion(bf16[4096,1024]{1,0:T(8,128)(2,1)} %bitcast.76, bf16[1,512,4096]{2,1,0:T(8,128)(2,1)} %all-gather.4.cloned.1.call-done), kind=kOutput, calls=%fused_computation.15 | convolution fusion | flops 4295491584 | bytes 13631488 | tf_op jit(solution)/shard_map/dot_general | solution.py:39
  106.5 0.9 fusion.43
  107.4 0.4 fusion.26
  107.8 3.5 %fusion.44 = (f32[2,512]{1,0:T(2,128)S(1)}, f32[2,512,512]{1,2,0:T(8,128)}) fusion(pred[512,512]{0,1:T(8,128)(4,1)S(1)} %broadcast_compare_fusion, bf16[512,2,256]{0,2,1:T(8,128)(2,1)} %bitcast.82, bf16[64,2,8,256]{3,2,1,0:T(8,128)(2,1)} %bitcast.85), kind=kOutput, calls=%fused_computation.46 | convolution fusion | flops 270533120 | bytes 3411968 | tf_op jit(solution)/shard_map/sub | solution.py:14
  111.3 2.9 %convolution_convert_fusion.1 = bf16[2,512,256]{1,2,0:T(8,128)(2,1)} fusion(bf16[512,2,256]{0,2,1:T(8,128)(2,1)S(1)} %bitcast.79, f32[2,512,512]{1,2,0:T(8,128)} %get-tuple-element.7, f32[2,512]{1,0:T(2,128)S(1)} %get-tuple-element.6), kind=kOutput, calls=%fused_computation.17 | convolution fusion | flops 269746176 | bytes 3149824 | tf_op jit(solution)/shard_map/hqk,qhd->khd/dot_general | solution.py:20
  114.1 4.2 %fusion.13 = bf16[2,512,256]{1,2,0:T(8,128)(2,1)} fusion(bf16[512,2,256]{0,2,1:T(8,128)(2,1)} %bitcast.83, f32[2,512,512]{2,1,0:T(8,128)S(1)} %fusion.26, f32[2,512,512]{1,2,0:T(8,128)} %get-tuple-element.7, f32[2,512]{1,0:T(2,128)S(1)} %get-tuple-element.6), kind=kOutput, calls=%fused_computation.16 | convolution fusion | flops 272369152 | bytes 5246976 | tf_op jit(solution)/shard_map/hqk,qhd->khd/dot_general | solution.py:26
  118.3 10.4 %fusion.2 = bf16[4096,512]{0,1:T(8,128)(2,1)} fusion(bf16[4096,1024]{1,0:T(8,128)(2,1)} %bitcast.77, bf16[512,512]{0,1:T(8,128)(2,1)S(1)} %bitcast.88, bf16[512,512]{0,1:T(8,128)(2,1)} %bitcast.89), kind=kOutput, calls=%fused_computation.3 | convolution fusion | flops 4299161600 | bytes 13631488 | tf_op jit(solution)/shard_map/dot_general | solution.py:58
  128.7 0.0 reduce-scatter.3.cloned.1.call-update
  128.8 0.0 reduce-scatter.5.cloned.1.call-start
  128.8 57.9 %reduce-scatter.3.cloned.1.call-done = bf16[256,512]{0,1:T(8,128)(2,1)} async-done(((bf16[4096,512]{0,1:T(8,128)(2,1)}), bf16[256,512]{0,1:T(8,128)(2,1)}) %reduce-scatter.3.cloned.1.call-update) | async-done | bytes 262160 | tf_op jit(solution)/shard_map/reduce_scatter | solution.py:57
  186.7 0.0 reduce-scatter.5.cloned.1.call-update
  186.7 0.5 convolution_convert_fusion.2
  187.2 1.0 copy.19
  188.2 77.0 %reduce-scatter.5.cloned.1.call-done = bf16[256,64]{0,1:T(8,128)(2,1)} async-done(((bf16[256,512]{0,1:T(8,128)(2,1)}), bf16[256,64]{0,1:T(8,128)(2,1)}) %reduce-scatter.5.cloned.1.call-update) | async-done | bytes 32784 | tf_op jit(solution)/shard_map/reduce_scatter | solution.py:66
  265.3 1.4 convert_bitcast_fusion
  (8 shorter events, 0.0 us)
Async XLA Ops:
  7.2 90.2 %all-gather.4.cloned.1.call-start = ((), (), s32[]{:S(2)}) async-start(), calls=%async_computation.4 | async-start | bytes 4456448 | tf_op jit(solution)/shard_map/all_gather | solution.py:40
  38.6 148.1 %reduce-scatter.3.cloned.1.call-start = ((), (), s32[]{:S(2)}) async-start(), calls=%async_computation.2 | async-start | bytes 4456448 | tf_op jit(solution)/shard_map/reduce_scatter | solution.py:57
  42.0 9.5 %copy-start = (s32[1,512]{1,0:T(1,128)S(1)}, s32[1,512]{1,0:T(1,128)}, u32[]{:S(2)}) copy-start(s32[1,512]{1,0:T(1,128)} %param.11) | copy-start | bytes 6148
  42.0 9.5 %copy-start.1 = (s32[1,512]{1,0:T(1,128)S(1)}, s32[1,512]{1,0:T(1,128)}, u32[]{:S(2)}) copy-start(s32[1,512]{1,0:T(1,128)} %param.10) | copy-start | bytes 6148
  114.1 4.2 %copy-start.2 = (bf16[2,512,256]{1,2,0:T(8,128)(2,1)S(1)}, bf16[2,512,256]{1,2,0:T(8,128)(2,1)}, u32[]{:S(2)}) copy-start(bf16[2,512,256]{1,2,0:T(8,128)(2,1)} %convolution_convert_fusion.1) | copy-start | bytes 1572868
  128.7 58.0 %copy-start.3 = (f32[2,512,512]{1,2,0:T(8,128)S(1)}, f32[2,512,512]{1,2,0:T(8,128)}, u32[]{:S(2)}) copy-start(f32[2,512,512]{1,2,0:T(8,128)} %get-tuple-element.7) | copy-start | bytes 6291460
  128.8 136.5 %reduce-scatter.5.cloned.1.call-start = ((), (), s32[]{:S(2)}) async-start(), calls=%async_computation.3 | async-start | bytes 294912 | tf_op jit(solution)/shard_map/reduce_scatter | solution.py:66
Sparse Core Ops, SparseCore 0:
  38.7 58.5 all-gather.3
  128.9 57.7 reduce-scatter.2
  190.5 74.6 reduce-scatter.4
where the time goes:
time: 274 us; the launch traced here: 273 us
  waiting for transfers between devices  181 us (66%)
  blocking collectives  31.4 us (11%)
  matrix products  31 us (11%)
  local copies, waits for them, and re-layouts  14.7 us (5%)
  between operations  13.8 us (5%)
    reduce_scatter x1, waiting for transfers between devices, per_device(): lax.psum_scatter(feature_share, 'mp', scatter_dimension=1, tiled=True)  77 us
    reduce_scatter x1, waiting for transfers between devices, per_device(): lax.psum_scatter(lax.dot_general(weight_rows, grad_both, (((1,), (1,)), (...  57.9 us
    all_gather x1, waiting for transfers between devices, per_device(): lax.all_gather(all_tokens, 'section', axis=1, tiled=True)  45.6 us
    all_gather x1, blocking collectives, per_device(): all_tokens = lax.all_gather(shard_rows, 'mp', axis=0, tiled=True)  31.4 us
    unnamed x10, local copies, waits for them, and re-layouts  10.5 us
    dot_general x1, matrix products, per_device(): lax.dot_general(weight_rows, grad_both, (((1,), (1,)), ((), ())), preferr...  10.4 us
    dot_general x1, matrix products, per_device(): jnp.dot(lax.all_gather(all_tokens, 'section', axis=1, tiled=True), weight...  9.14 us
  transfers between devices with their start and end apart: 3, of which 3 were waited for; matrix products, arithmetic and copies ran while one was open for 5% of the time, Pallas kernels for 0%

commit v1 on v0

v1 whole, which is shorter than its diff:
```python
import functools

import jax
import jax.numpy as jnp
from jax import lax
from jax.experimental import pallas as pl
from jax.experimental.pallas import tpu as pltpu
from jax.sharding import Mesh, PartitionSpec as P

HD = 256
NZ, NC, NX, NY, ND = 8, 2, 4, 2, 2
TB = 64
FB = 256
VMEM = 48 << 20


def project_kernel(core_ref, *refs):
    own, other, w_ref, out_ref, acc_ref = refs[:8], refs[8:16], refs[16], refs[17], refs[18]
    step = pl.program_id(0)
    core = core_ref[0]
    own_rows = jnp.concatenate([r[0] for r in own], axis=0)
    other_rows = jnp.concatenate([r[0] for r in other], axis=0)
    w_own = w_ref[pl.ds(pl.multiple_of(core * FB, FB), FB), :]
    w_other = w_ref[pl.ds(pl.multiple_of((1 - core) * FB, FB), FB), :]
    part = jnp.dot(own_rows, w_own, preferred_element_type=jnp.float32)
    part = part + jnp.dot(other_rows, w_other, preferred_element_type=jnp.float32)

    @pl.when(step == 0)
    def _():
        acc_ref[...] = part

    @pl.when(step > 0)
    def _():
        acc_ref[...] = acc_ref[...] + part

    @pl.when(step == NZ - 1)
    def _():
        out_ref[...] = acc_ref[...].astype(jnp.bfloat16)


def project(core, own, other, weight):
    width = weight.shape[1]
    rows = 8 * TB
    block = pl.BlockSpec((1, TB, FB), lambda z, c: (z, 0, 0))
    return pl.pallas_call(
        project_kernel,
        grid_spec=pltpu.PrefetchScalarGridSpec(
            num_scalar_prefetch=1,
            grid=(NZ,),
            in_specs=[block] * 16 + [pl.BlockSpec((2 * FB, width), lambda z, c: (z, 0))],
            out_specs=pl.BlockSpec((rows, width), lambda z, c: (0, 0)),
            scratch_shapes=[pltpu.VMEM((rows, width), jnp.float32)],
        ),
        out_shape=jax.ShapeDtypeStruct((rows, width), jnp.bfloat16),
        compiler_params=pltpu.CompilerParams(vmem_limit_bytes=VMEM),
        name="project",
    )(core, *own, *other, weight)


NT = (((1,), (1,)), ((), ()))
TN = (((0,), (0,)), ((), ()))


def attend_kernel(q_ref, g_ref, k_ref, v_ref, es_ref, ds_ref, ctx_ref, gk_ref, gv_ref):
    scale = HD ** -0.5
    q, g, k, v = q_ref[...], g_ref[...], k_ref[...], v_ref[...]
    same = es_ref[...] == ds_ref[...]
    scores = lax.dot_general(k, q, NT, preferred_element_type=jnp.float32) * scale
    scores = jnp.where(same, scores, -1e30)
    top = jnp.max(scores, axis=0, keepdims=True)
    raised = jnp.exp(scores - top)
    probs = raised / jnp.sum(raised, axis=0, keepdims=True)
    low = probs.astype(jnp.bfloat16)
    ctx_ref[...] = lax.dot_general(low, v, TN, preferred_element_type=jnp.float32).astype(jnp.bfloat16)
    gv_ref[...] = jnp.dot(low, g, preferred_element_type=jnp.float32).astype(jnp.bfloat16)
    gp = lax.dot_general(v, g, NT, preferred_element_type=jnp.float32)
    inner = jnp.sum(probs * gp, axis=0, keepdims=True)
    gs = (probs * (gp - inner) * scale).astype(jnp.bfloat16)
    gk_ref[...] = jnp.dot(gs, q, preferred_element_type=jnp.float32).astype(jnp.bfloat16)


def attend(query, grad, key_values, enc_col, dec_row):
    dec, width = query.shape
    enc = key_values.shape[0]
    heads = width // HD
    head = pl.BlockSpec((dec, HD), lambda h: (0, h))
    key = pl.BlockSpec((enc, HD), lambda h: (0, h))
    value = pl.BlockSpec((enc, HD), lambda h: (0, heads + h))
    return pl.pallas_call(
        attend_kernel,
        grid=(heads,),
        in_specs=[head, head, key, value, pl.BlockSpec((enc, 1), lambda h: (0, 0)), pl.BlockSpec((1, dec), lambda h: (0, 0))],
        out_specs=[head, key, key],
        out_shape=[
            jax.ShapeDtypeStruct((dec, width), jnp.bfloat16),
            jax.ShapeDtypeStruct((enc, width), jnp.bfloat16),
            jax.ShapeDtypeStruct((enc, width), jnp.bfloat16),
        ],
        compiler_params=pltpu.CompilerParams(vmem_limit_bytes=VMEM),
        name="attend",
    )(query, grad, key_values, key_values, enc_col, dec_row)


def spread_other_kernel(core_ref, gk_ref, gv_ref, w_ref, first_ref, second_ref):
    core = core_ref[0]
    width = gk_ref.shape[1]
    rows = pl.ds(pl.multiple_of((1 - core) * FB, FB), FB)
    out = lax.dot_general(gk_ref[...], w_ref[rows, :width], NT, preferred_element_type=jnp.float32)
    out = out + lax.dot_general(gv_ref[...], w_ref[rows, width:], NT, preferred_element_type=jnp.float32)
    out = out.astype(jnp.bfloat16).reshape(8, TB, FB)
    first_ref[:, 0] = out[:4]
    second_ref[:, 0] = out[4:]


def spread_other(core, grad_keys, grad_values, weight):
    rows, width = grad_keys.shape
    half = pl.BlockSpec((4, 1, TB, FB), lambda z, c: (0, z, 0, 0))
    whole = pl.BlockSpec((rows, width), lambda z, c: (0, 0))
    shape = jax.ShapeDtypeStruct((4, NZ, TB, FB), jnp.bfloat16)
    return pl.pallas_call(
        spread_other_kernel,
        grid_spec=pltpu.PrefetchScalarGridSpec(
            num_scalar_prefetch=1,
            grid=(NZ,),
            in_specs=[whole, whole, pl.BlockSpec((2 * FB, 2 * width), lambda z, c: (z, 0))],
            out_specs=[half, half],
        ),
        out_shape=[shape, shape],
        compiler_params=pltpu.CompilerParams(vmem_limit_bytes=VMEM),
        name="spread_other",
    )(core, grad_keys, grad_values, weight)


def spread_own_kernel(core_ref, gk_ref, gv_ref, w_ref, twin_ref, *out_refs):
    core = core_ref[0]
    width = gk_ref.shape[1]
    rows = pl.ds(pl.multiple_of(core * FB, FB), FB)
    out = lax.dot_general(gk_ref[...], w_ref[rows, :width], NT, preferred_element_type=jnp.float32)
    out = out + lax.dot_general(gv_ref[...], w_ref[rows, width:], NT, preferred_element_type=jnp.float32)
    out = out.reshape(4, TB, FB)
    for i in range(4):
        out_refs[i][0] = (out[i] + twin_ref[i, 0].astype(jnp.float32)).astype(jnp.bfloat16)


def spread_own(core, grad_keys, grad_values, weight, twin, which):
    rows, width = grad_keys.shape
    rows = rows // 2
    half = pl.BlockSpec((4, 1, TB, FB), lambda z, c: (0, z, 0, 0))
    part = pl.BlockSpec((rows, width), lambda z, c: (which, 0))
    shape = jax.ShapeDtypeStruct((NZ, TB, FB), jnp.bfloat16)
    return pl.pallas_call(
        spread_own_kernel,
        grid_spec=pltpu.PrefetchScalarGridSpec(
            num_scalar_prefetch=1,
            grid=(NZ,),
            in_specs=[part, part, pl.BlockSpec((2 * FB, 2 * width), lambda z, c: (z, 0)), half],
            out_specs=[pl.BlockSpec((1, TB, FB), lambda z, c: (z, 0, 0))] * 4,
        ),
        out_shape=[shape] * 4,
        compiler_params=pltpu.CompilerParams(vmem_limit_bytes=VMEM),
        name="spread_own",
    )(core, grad_keys, grad_values, weight, twin)


def shift(value, axis, size, by):
    return lax.ppermute(value, axis, [(i, (i + by) % size) for i in range(size)])


def total(parts):
    return functools.reduce(jnp.add, [p.astype(jnp.float32) for p in parts])


def per_device(enc_out, kv_weight, dec_query, ctx_grad, enc_seg, dec_seg):
    width = kv_weight.shape[3]
    weight = kv_weight[0].reshape(kv_weight.shape[1], 2 * width)
    core = lax.axis_index("c").reshape(1)
    x, y = lax.axis_index("x"), lax.axis_index("y")

    blocks = jnp.stack([((x + j) % NX) * NY + (1 - y if far else y) for far in (1, 0) for j in range(NX)])
    enc_col = enc_seg[0].reshape(8, TB)[blocks].reshape(8 * TB, 1)

    mine = enc_out[0]
    near = lax.all_to_all(jnp.broadcast_to(mine[None], (NZ, TB, FB)), "z", 0, 0)
    far = shift(near, "y", NY, 1)
    own = [far, None, None, None, near, None, None, None]
    for j in (2, 1, 3):
        own[4 + j] = shift(near, "x", NX, -j)
    for j in (2, 1, 3):
        own[j] = shift(far, "x", NX, -j)
    other = [shift(v, "c", NC, 1) for v in own]
    key_values = project(core, own, other, weight)

    context, grad_keys, grad_values = attend(dec_query[0, 0], ctx_grad[0, 0], key_values, enc_col, dec_seg)

    first, second = spread_other(core, grad_keys, grad_values, weight)
    first, second = shift(first, "c", NC, 1), shift(second, "c", NC, 1)
    away = spread_own(core, grad_keys, grad_values, weight, first, 0)
    home = spread_own(core, grad_keys, grad_values, weight, second, 1)
    away = [away[0]] + [shift(away[j], "x", NX, j) for j in (1, 2, 3)]
    home = [home[0]] + [shift(home[j], "x", NX, j) for j in (1, 2, 3)]
    crossed = shift(total(away).astype(jnp.bfloat16), "y", NY, 1)
    planes = total(home + [crossed]).astype(jnp.bfloat16)
    planes = lax.all_to_all(planes, "z", 0, 0)
    owned = jnp.sum(planes.astype(jnp.float32), axis=0)
    return context[None, None], owned[None]


def solution(mesh):
    fine = Mesh(mesh.devices.reshape(NZ, NC, NX, NY, ND), ("z", "c", "x", "y", "d"))
    section, mp = ("z", "c"), ("x", "y")
    placed = (
        P("d", mp, section),
        P(section, None, None, mp),
        P(section, "d", None, mp),
        P(section, "d", None, mp),
        P("d", None),
        P("d", None),
    )
    return jax.shard_map(
        per_device,
        mesh=fine,
        in_specs=placed,
        out_specs=(P(section, "d", None, mp), P("d", mp, section)),
        check_vma=False,
    )
```

time: 274 us -> 136 us (0.50)
  waiting for transfers between devices: 181 us -> 23.2 us
  Pallas kernels: 0 us -> 35.7 us
  matrix products: 31 us -> 0 us
  starting transfers between devices: 0.12 us -> 27.2 us
  between operations: 13.8 us -> 0.78 us
    reduce_scatter x2 -> x0, waiting for transfers between devices: 135 us -> none  [the longest x1 77 us: per_device(): lax.psum_scatter(feature_share, 'mp', scatter_dimension=1, tiled=True)]
    all_gather x1 -> x0, waiting for transfers between devices: 45.6 us -> none  [per_device(): lax.all_gather(all_tokens, 'section', axis=1, tiled=True)]
    pallas_call x0 -> x5, Pallas kernels: none -> 35.7 us  [the longest x2 13.8 us: spread_own(): pl.pallas_call(spread_own_kernel, grid_spec=pltpu.PrefetchScalarGridSpec(...]
    all_to_all x0 -> x2, blocking collectives: none -> 33.2 us  [the longest x1 19.2 us: per_device(): near = lax.all_to_all(jnp.broadcast_to(mine[None], (NZ, TB, FB)), 'z', 0, 0)]
    all_gather x1 -> x0, blocking collectives: 31.4 us -> none  [per_device(): all_tokens = lax.all_gather(shard_rows, 'mp', axis=0, tiled=True)]
    dot_general x6 -> x0, matrix products: 27.5 us -> none  [the longest x1 10.4 us: per_device(): lax.dot_general(weight_rows, grad_both, (((1,), (1,)), ((), ())), preferr...]
    ppermute x0 -> x24, starting transfers between devices: none -> 27.2 us  [shift(): lax.ppermute(value, axis, [(i, (i + by) % size) for i in range(size)])]
    ppermute x0 -> x24, waiting for transfers between devices: none -> 23.2 us  [shift(): lax.ppermute(value, axis, [(i, (i + by) % size) for i in range(size)])]
  transfers between devices with their start and end apart: 3 -> 24, of which waited for: 3 -> 8; matrix products, arithmetic and copies ran while one was open for 5% -> 9% of each run, Pallas kernels for 0% -> 10%
where the time goes in v1:
time: 136 us; the launch traced here: 135 us
  Pallas kernels  35.7 us (26%)
  blocking collectives  33.2 us (24%)
  starting transfers between devices  27.2 us (20%)
  waiting for transfers between devices  23.2 us (17%)
  local copies, waits for them, and re-layouts  13.3 us (10%)
  other arithmetic  1.66 us (1%)
    ppermute x24, starting transfers between devices, shift(): lax.ppermute(value, axis, [(i, (i + by) % size) for i in range(size)])  27.2 us
    ppermute x24, waiting for transfers between devices, shift(): lax.ppermute(value, axis, [(i, (i + by) % size) for i in range(size)])  23.2 us
    all_to_all x1, blocking collectives, per_device(): near = lax.all_to_all(jnp.broadcast_to(mine[None], (NZ, TB, FB)), 'z', 0, 0)  19.2 us
    all_to_all x1, blocking collectives, per_device(): planes = lax.all_to_all(planes, 'z', 0, 0)  14.1 us
    pallas_call x2, Pallas kernels, spread_own(): pl.pallas_call(spread_own_kernel, grid_spec=pltpu.PrefetchScalarGridSpec(...  13.8 us
    unnamed x14, local copies, waits for them, and re-layouts  11.6 us
    pallas_call x1, Pallas kernels, project(): pl.pallas_call(project_kernel, grid_spec=pltpu.PrefetchScalarGridSpec(num...  10.4 us
    pallas_call x1, Pallas kernels, spread_other(): pl.pallas_call(spread_other_kernel, grid_spec=pltpu.PrefetchScalarGridSpe...  7.63 us
  transfers between devices with their start and end apart: 24, of which 8 were waited for; matrix products, arithmetic and copies ran while one was open for 9% of the time, Pallas kernels for 10%

profile of v1, /device:TPU:1, one launch (start us, length us, event | category | flops | bytes accessed | tf_op | source)
XLA Modules:
  0.0 135.1 jit_solution(13020136790914108010)
XLA Ops:
  1.4 19.2 %all_to_all.10.refs_4_ = bf16[8,64,256]{2,1,0:T(8,128)(2,1)S(1)} all-to-all(bf16[8,64,256]{2,1,0:T(8,128)(2,1)S(1)} %broadcast_in_dim.15), channel_id=1, replica_groups=mesh['z'=8,'c'=2,'x'=4,'y'=2,'d'=2] {'z'}, dimensions={0} | all-to-all | bytes 524288 | tf_op jit(solution)/shard_map/all_to_all | solution.py:183
  20.6 2.9 %collective-permute-start = (bf16[8,64,256]{2,1,0:T(8,128)(2,1)S(1)}, bf16[8,64,256]{2,1,0:T(8,128)(2,1)S(1)}, u32[]{:S(2)}, u32[]{:S(2)}) collective-permute-start(bf16[8,64,256]{2,1,0:T(8,128)(2,1)S(1)} %all_to_all.10.refs_4_), channel_id=1, source_target_pairs={{0,2},{2,0},{1,3},{3,1},{4,6},{6,4},{5,7},{7,5},{8,10},{10,8},{9,1... | collective-permute-start | bytes 786440 | tf_op jit(solution)/shard_map/ppermute | solution.py:166
  23.5 2.5 %collective-permute-start.4 = (bf16[8,64,256]{2,1,0:T(8,128)(2,1)S(1)}, bf16[8,64,256]{2,1,0:T(8,128)(2,1)S(1)}, u32[]{:S(2)}, u32[]{:S(2)}) collective-permute-start(bf16[8,64,256]{2,1,0:T(8,128)(2,1)S(1)} %all_to_all.10.refs_4_), channel_id=1, source_target_pairs={{0,12},{4,0},{8,4},{12,8},{1,13},{5,1},{9,5},{13,9},{2,14},{6,2},{... | collective-permute-start | bytes 786440 | tf_op jit(solution)/shard_map/ppermute | solution.py:166
  27.1 3.6 %collective-permute-start.11 = (bf16[8,64,256]{2,1,0:T(8,128)(2,1)S(1)}, bf16[8,64,256]{2,1,0:T(8,128)(2,1)S(1)}, u32[]{:S(2)}, u32[]{:S(2)}) collective-permute-start(bf16[8,64,256]{2,1,0:T(8,128)(2,1)S(1)} %all_to_all.10.refs_4_), channel_id=1, source_target_pairs={{0,16},{16,0},{1,17},{17,1},{2,18},{18,2},{3,19},{19,3},{4,20},{20... | collective-permute-start | bytes 786440 | tf_op jit(solution)/shard_map/ppermute | solution.py:166
  30.7 2.1 %collective-permute-start.1 = (bf16[8,64,256]{2,1,0:T(8,128)(2,1)S(1)}, bf16[8,64,256]{2,1,0:T(8,128)(2,1)S(1)}, u32[]{:S(2)}, u32[]{:S(2)}) collective-permute-start(bf16[8,64,256]{2,1,0:T(8,128)(2,1)S(1)} %collective-permute-done.refs_0_), channel_id=1, source_target_pairs={{0,12},{4,0},{8,4},{12,8},{1,13},{5,1},{9,5},{13,9},{2,14},{6,2},{... | collective-permute-start | bytes 786440 | tf_op jit(solution)/shard_map/ppermute | solution.py:166
  32.8 1.2 collective-permute-start.2
  34.0 2.3 %collective-permute-start.3 = (bf16[8,64,256]{2,1,0:T(8,128)(2,1)S(1)}, bf16[8,64,256]{2,1,0:T(8,128)(2,1)}, u32[]{:S(2)}, u32[]{:S(2)}) collective-permute-start(bf16[8,64,256]{2,1,0:T(8,128)(2,1)S(1)} %collective-permute-done.refs_0_), channel_id=1, source_target_pairs={{0,4},{4,8},{8,12},{12,0},{1,5},{5,9},{9,13},{13,1},{2,6},{6,10},{... | collective-permute-start | bytes 786440 | tf_op jit(solution)/shard_map/ppermute | solution.py:166
  36.3 6.6 %collective-permute-done.6.refs_7_ = bf16[8,64,256]{2,1,0:T(8,128)(2,1)S(1)} collective-permute-done((bf16[8,64,256]{2,1,0:T(8,128)(2,1)S(1)}, bf16[8,64,256]{2,1,0:T(8,128)(2,1)S(1)}, u32[]{:S(2)}, u32[]{:S(2)}) %collective-permute-start.6) | collective-permute-done | bytes 262176 | tf_op jit(solution)/shard_map/ppermute | solution.py:166
  42.8 3.1 %collective-permute-start.7 = (bf16[8,64,256]{2,1,0:T(8,128)(2,1)S(1)}, bf16[8,64,256]{2,1,0:T(8,128)(2,1)S(1)}, u32[]{:S(2)}, u32[]{:S(2)}) collective-permute-start(bf16[8,64,256]{2,1,0:T(8,128)(2,1)S(1)} %collective-permute-done.refs_0_), channel_id=1, source_target_pairs={{0,16},{16,0},{1,17},{17,1},{2,18},{18,2},{3,19},{19,3},{4,20},{20... | collective-permute-start | bytes 786440 | tf_op jit(solution)/shard_map/ppermute | solution.py:166
  46.0 9.4 %copy.9 = bf16[512,8,2,512]{3,1,2,0:T(8,128)(2,1)} copy(bf16[512,8,2,512]{3,2,1,0:T(2,128)(2,1)} %bitcast.25) | data formatting | bytes 16777216
  61.7 10.4 %project.1.k_ref.v_ref = bf16[512,1024]{1,0:T(8,128)(2,1)S(1)} custom-call(s32[1]{0:T(128)} %bitcast.2.core_ref, bf16[8,64,256]{2,1,0:T(8,128)(2,1)S(1)} %collective-permute-done.refs_0_, bf16[8,64,256]{2,1,0:T(8,128)(2,1)S(1)} %collective-permute-done.1.refs_1_, bf16[8,64,256]{2,1,0:T(8,128)(2,1)S(1)} %collective-permute-done.2.refs_2_, ...), custom_call_target="tpu_custom_call" | custom-call | tf_op jit(solution)/shard_map/project/pallas_call | solution.py:45
  72.1 3.9 %attend.1 = (bf16[512,512]{1,0:T(8,128)(2,1)}, bf16[512,512]{1,0:T(8,128)(2,1)S(1)}, bf16[512,512]{1,0:T(8,128)(2,1)S(1)}) custom-call(bf16[512,512]{1,0:T(8,128)(2,1)S(1)} %bitcast.19, bf16[512,512]{1,0:T(8,128)(2,1)S(1)} %bitcast.20, bf16[512,1024]{1,0:T(8,128)(2,1)S(1)} %project.1.k_ref.v_ref, bf16[512,1024]{1,0:T(8,128)(2,1)S(1)} %project.1.k_ref.v_ref, ...), custom_call_target="tpu_custom_call" | custom-call | tf_op jit(solution)/shard_map/attend/pallas_call | solution.py:89
  76.1 7.6 %spread_other.1 = (bf16[4,8,64,256]{3,2,1,0:T(8,128)(2,1)S(1)}, bf16[4,8,64,256]{3,2,1,0:T(8,128)(2,1)S(1)}) custom-call(s32[1]{0:T(128)} %bitcast.2.core_ref, bf16[512,512]{1,0:T(8,128)(2,1)S(1)} %get-tuple-element.16.gk_ref, bf16[512,512]{1,0:T(8,128)(2,1)S(1)} %get-tuple-element.17.gv_ref, bf16[4096,1024]{1,0:T(8,128)(2,1)} %bitcast.22), custom_call_target="tpu_custom_call" | custom-call | tf_op jit(solution)/shard_map/spread_other/pallas_call | solution.py:120
  84.3 2.1 %collective-permute-done.19.twin_ref = bf16[4,8,64,256]{3,2,1,0:T(8,128)(2,1)S(1)} collective-permute-done((bf16[4,8,64,256]{3,2,1,0:T(8,128)(2,1)S(1)}, bf16[4,8,64,256]{3,2,1,0:T(8,128)(2,1)S(1)}, u32[]{:S(2)}, u32[]{:S(2)}) %collective-permute-start.19) | collective-permute-done | bytes 1048608 | tf_op jit(solution)/shard_map/ppermute | solution.py:166
  86.5 6.9 %spread_own.3 = (bf16[8,64,256]{2,1,0:T(8,128)(2,1)S(1)}, bf16[8,64,256]{2,1,0:T(8,128)(2,1)S(1)}, bf16[8,64,256]{2,1,0:T(8,128)(2,1)S(1)}, bf16[8,64,256]{2,1,0:T(8,128)(2,1)S(1)}) custom-call(s32[1]{0:T(128)} %bitcast.2.core_ref, bf16[512,512]{1,0:T(8,128)(2,1)S(1)} %get-tuple-element.16.gk_ref, bf16[512,512]{1,0:T(8,128)(2,1)S(1)} %get-tuple-element.17.gv_ref, ...), custom_call_target="tpu_custom_call" | custom-call | tf_op jit(solution)/shard_map/spread_own/pallas_call | solution.py:151
  93.5 1.3 collective-permute-start.21
  95.5 6.9 %spread_own.2 = (bf16[8,64,256]{2,1,0:T(8,128)(2,1)S(1)}, bf16[8,64,256]{2,1,0:T(8,128)(2,1)S(1)}, bf16[8,64,256]{2,1,0:T(8,128)(2,1)S(1)}, bf16[8,64,256]{2,1,0:T(8,128)(2,1)S(1)}) custom-call(s32[1]{0:T(128)} %bitcast.2.core_ref, bf16[512,512]{1,0:T(8,128)(2,1)S(1)} %get-tuple-element.16.gk_ref, bf16[512,512]{1,0:T(8,128)(2,1)S(1)} %get-tuple-element.17.gv_ref, ...), custom_call_target="tpu_custom_call" | custom-call | tf_op jit(solution)/shard_map/spread_own/pallas_call | solution.py:151
  102.4 2.0 %collective-permute-start.18 = (bf16[8,64,256]{2,1,0:T(8,128)(2,1)S(1)}, bf16[8,64,256]{2,1,0:T(8,128)(2,1)S(1)}, u32[]{:S(2)}, u32[]{:S(2)}) collective-permute-start(bf16[8,64,256]{2,1,0:T(8,128)(2,1)S(1)} %get-tuple-element.22), channel_id=1, source_target_pairs={{0,12},{4,0},{8,4},{12,8},{1,13},{5,1},{9,5},{13,9},{2,14},{6,2},{... | collective-permute-start | bytes 786440 | tf_op jit(solution)/shard_map/ppermute | solution.py:166
  104.4 1.2 collective-permute-start.17
  106.4 2.8 %collective-permute-done.20 = bf16[8,64,256]{2,1,0:T(8,128)(2,1)S(1)} collective-permute-done((bf16[8,64,256]{2,1,0:T(8,128)(2,1)S(1)}, bf16[8,64,256]{2,1,0:T(8,128)(2,1)S(1)}, u32[]{:S(2)}, u32[]{:S(2)}) %collective-permute-start.20) | collective-permute-done | bytes 262176 | tf_op jit(solution)/shard_map/ppermute | solution.py:166
  109.4 3.0 %collective-permute-done.18 = bf16[8,64,256]{2,1,0:T(8,128)(2,1)S(1)} collective-permute-done((bf16[8,64,256]{2,1,0:T(8,128)(2,1)S(1)}, bf16[8,64,256]{2,1,0:T(8,128)(2,1)S(1)}, u32[]{:S(2)}, u32[]{:S(2)}) %collective-permute-start.18) | collective-permute-done | bytes 262176 | tf_op jit(solution)/shard_map/ppermute | solution.py:166
  112.5 1.1 collective-permute-done.17
  113.6 6.6 %collective-permute-done.16 = bf16[8,64,256]{2,1,0:T(8,128)(2,1)S(1)} collective-permute-done((bf16[8,64,256]{2,1,0:T(8,128)(2,1)S(1)}, bf16[8,64,256]{2,1,0:T(8,128)(2,1)S(1)}, u32[]{:S(2)}, u32[]{:S(2)}) %collective-permute-start.16) | collective-permute-done | bytes 262176 | tf_op jit(solution)/shard_map/ppermute | solution.py:166
  120.4 14.1 %all_to_all.11 = bf16[8,64,256]{2,1,0:T(8,128)(2,1)S(1)} all-to-all(bf16[8,64,256]{2,1,0:T(8,128)(2,1)S(1)} %add_convert_fusion), channel_id=1, replica_groups=mesh['z'=8,'c'=2,'x'=4,'y'=2,'d'=2] {'z'}, dimensions={0} | all-to-all | bytes 524288 | tf_op jit(solution)/shard_map/all_to_all | solution.py:203
  (56 shorter events, 11.6 us)
Async XLA Ops:
  20.6 10.1 %collective-permute-start = (bf16[8,64,256]{2,1,0:T(8,128)(2,1)S(1)}, bf16[8,64,256]{2,1,0:T(8,128)(2,1)S(1)}, u32[]{:S(2)}, u32[]{:S(2)}) collective-permute-start(bf16[8,64,256]{2,1,0:T(8,128)(2,1)S(1)} %all_to_all.10.refs_4_), channel_id=1, source_target_pairs={{0,2},{2,0},{1,3},{3,1},{4,6},{6,4},{5,7},{7,5},{8,10},{10,8},{9,1... | collective-permute-start | bytes 786440 | tf_op jit(solution)/shard_map/ppermute | solution.py:166
  23.5 9.3 %collective-permute-start.4 = (bf16[8,64,256]{2,1,0:T(8,128)(2,1)S(1)}, bf16[8,64,256]{2,1,0:T(8,128)(2,1)S(1)}, u32[]{:S(2)}, u32[]{:S(2)}) collective-permute-start(bf16[8,64,256]{2,1,0:T(8,128)(2,1)S(1)} %all_to_all.10.refs_4_), channel_id=1, source_target_pairs={{0,12},{4,0},{8,4},{12,8},{1,13},{5,1},{9,5},{13,9},{2,14},{6,2},{... | collective-permute-start | bytes 786440 | tf_op jit(solution)/shard_map/ppermute | solution.py:166
  26.0 8.0 %collective-permute-start.5 = (bf16[8,64,256]{2,1,0:T(8,128)(2,1)S(1)}, bf16[8,64,256]{2,1,0:T(8,128)(2,1)S(1)}, u32[]{:S(2)}, u32[]{:S(2)}) collective-permute-start(bf16[8,64,256]{2,1,0:T(8,128)(2,1)S(1)} %all_to_all.10.refs_4_), channel_id=1, source_target_pairs={{0,8},{4,12},{8,0},{12,4},{1,9},{5,13},{9,1},{13,5},{2,10},{6,14},... | collective-permute-start | bytes 786440 | tf_op jit(solution)/shard_map/ppermute | solution.py:166
  26.5 16.3 %collective-permute-start.6 = (bf16[8,64,256]{2,1,0:T(8,128)(2,1)S(1)}, bf16[8,64,256]{2,1,0:T(8,128)(2,1)S(1)}, u32[]{:S(2)}, u32[]{:S(2)}) collective-permute-start(bf16[8,64,256]{2,1,0:T(8,128)(2,1)S(1)} %all_to_all.10.refs_4_), channel_id=1, source_target_pairs={{0,4},{4,8},{8,12},{12,0},{1,5},{5,9},{9,13},{13,1},{2,6},{6,10},{... | collective-permute-start | bytes 786440 | tf_op jit(solution)/shard_map/ppermute | solution.py:166
  27.1 18.8 %collective-permute-start.11 = (bf16[8,64,256]{2,1,0:T(8,128)(2,1)S(1)}, bf16[8,64,256]{2,1,0:T(8,128)(2,1)S(1)}, u32[]{:S(2)}, u32[]{:S(2)}) collective-permute-start(bf16[8,64,256]{2,1,0:T(8,128)(2,1)S(1)} %all_to_all.10.refs_4_), channel_id=1, source_target_pairs={{0,16},{16,0},{1,17},{17,1},{2,18},{18,2},{3,19},{19,3},{4,20},{20... | collective-permute-start | bytes 786440 | tf_op jit(solution)/shard_map/ppermute | solution.py:166
  30.7 26.0 %collective-permute-start.1 = (bf16[8,64,256]{2,1,0:T(8,128)(2,1)S(1)}, bf16[8,64,256]{2,1,0:T(8,128)(2,1)S(1)}, u32[]{:S(2)}, u32[]{:S(2)}) collective-permute-start(bf16[8,64,256]{2,1,0:T(8,128)(2,1)S(1)} %collective-permute-done.refs_0_), channel_id=1, source_target_pairs={{0,12},{4,0},{8,4},{12,8},{1,13},{5,1},{9,5},{13,9},{2,14},{6,2},{... | collective-permute-start | bytes 786440 | tf_op jit(solution)/shard_map/ppermute | solution.py:166
  32.8 24.5 %collective-permute-start.2 = (bf16[8,64,256]{2,1,0:T(8,128)(2,1)S(1)}, bf16[8,64,256]{2,1,0:T(8,128)(2,1)S(1)}, u32[]{:S(2)}, u32[]{:S(2)}) collective-permute-start(bf16[8,64,256]{2,1,0:T(8,128)(2,1)S(1)} %collective-permute-done.refs_0_), channel_id=1, source_target_pairs={{0,8},{4,12},{8,0},{12,4},{1,9},{5,13},{9,1},{13,5},{2,10},{6,14},... | collective-permute-start | bytes 786440 | tf_op jit(solution)/shard_map/ppermute | solution.py:166
  34.0 23.4 %collective-permute-start.3 = (bf16[8,64,256]{2,1,0:T(8,128)(2,1)S(1)}, bf16[8,64,256]{2,1,0:T(8,128)(2,1)}, u32[]{:S(2)}, u32[]{:S(2)}) collective-permute-start(bf16[8,64,256]{2,1,0:T(8,128)(2,1)S(1)} %collective-permute-done.refs_0_), channel_id=1, source_target_pairs={{0,4},{4,8},{8,12},{12,0},{1,5},{5,9},{9,13},{13,1},{2,6},{6,10},{... | collective-permute-start | bytes 786440 | tf_op jit(solution)/shard_map/ppermute | solution.py:166
  42.8 15.0 %collective-permute-start.7 = (bf16[8,64,256]{2,1,0:T(8,128)(2,1)S(1)}, bf16[8,64,256]{2,1,0:T(8,128)(2,1)S(1)}, u32[]{:S(2)}, u32[]{:S(2)}) collective-permute-start(bf16[8,64,256]{2,1,0:T(8,128)(2,1)S(1)} %collective-permute-done.refs_0_), channel_id=1, source_target_pairs={{0,16},{16,0},{1,17},{17,1},{2,18},{18,2},{3,19},{19,3},{4,20},{20... | collective-permute-start | bytes 786440 | tf_op jit(solution)/shard_map/ppermute | solution.py:166
  45.9 12.7 %collective-permute-start.12 = (bf16[8,64,256]{2,1,0:T(8,128)(2,1)S(1)}, bf16[8,64,256]{2,1,0:T(8,128)(2,1)}, u32[]{:S(2)}, u32[]{:S(2)}) collective-permute-start(bf16[8,64,256]{2,1,0:T(8,128)(2,1)S(1)} %collective-permute-done.4.refs_5_), channel_id=1, source_target_pairs={{0,16},{16,0},{1,17},{17,1},{2,18},{18,2},{3,19},{19,3},{4,20},{20... | collective-permute-start | bytes 786440 | tf_op jit(solution)/shard_map/ppermute | solution.py:166
  56.7 3.1 %collective-permute-start.13 = (bf16[8,64,256]{2,1,0:T(8,128)(2,1)S(1)}, bf16[8,64,256]{2,1,0:T(8,128)(2,1)}, u32[]{:S(2)}, u32[]{:S(2)}) collective-permute-start(bf16[8,64,256]{2,1,0:T(8,128)(2,1)S(1)} %collective-permute-done.5.refs_6_), channel_id=1, source_target_pairs={{0,16},{16,0},{1,17},{17,1},{2,18},{18,2},{3,19},{19,3},{4,20},{20... | collective-permute-start | bytes 786440 | tf_op jit(solution)/shard_map/ppermute | solution.py:166
  57.3 2.5 %collective-permute-start.14 = (bf16[8,64,256]{2,1,0:T(8,128)(2,1)S(1)}, bf16[8,64,256]{2,1,0:T(8,128)(2,1)}, u32[]{:S(2)}, u32[]{:S(2)}) collective-permute-start(bf16[8,64,256]{2,1,0:T(8,128)(2,1)S(1)} %collective-permute-done.6.refs_7_), channel_id=1, source_target_pairs={{0,16},{16,0},{1,17},{17,1},{2,18},{18,2},{3,19},{19,3},{4,20},{20... | collective-permute-start | bytes 786440 | tf_op jit(solution)/shard_map/ppermute | solution.py:166
  57.4 2.4 %collective-permute-start.8 = (bf16[8,64,256]{2,1,0:T(8,128)(2,1)S(1)}, bf16[8,64,256]{2,1,0:T(8,128)(2,1)}, u32[]{:S(2)}, u32[]{:S(2)}) collective-permute-start(bf16[8,64,256]{2,1,0:T(8,128)(2,1)S(1)} %collective-permute-done.1.refs_1_), channel_id=1, source_target_pairs={{0,16},{16,0},{1,17},{17,1},{2,18},{18,2},{3,19},{19,3},{4,20},{20... | collective-permute-start | bytes 786440 | tf_op jit(solution)/shard_map/ppermute | solution.py:166
  58.5 1.7 %collective-permute-start.9 = (bf16[8,64,256]{2,1,0:T(8,128)(2,1)S(1)}, bf16[8,64,256]{2,1,0:T(8,128)(2,1)}, u32[]{:S(2)}, u32[]{:S(2)}) collective-permute-start(bf16[8,64,256]{2,1,0:T(8,128)(2,1)S(1)} %collective-permute-done.2.refs_2_), channel_id=1, source_target_pairs={{0,16},{16,0},{1,17},{17,1},{2,18},{18,2},{3,19},{19,3},{4,20},{20... | collective-permute-start | bytes 786440 | tf_op jit(solution)/shard_map/ppermute | solution.py:166
  58.6 2.1 %collective-permute-start.10 = (bf16[8,64,256]{2,1,0:T(8,128)(2,1)}, bf16[8,64,256]{2,1,0:T(8,128)(2,1)}, u32[]{:S(2)}, u32[]{:S(2)}) collective-permute-start(bf16[8,64,256]{2,1,0:T(8,128)(2,1)} %collective-permute-done.3.refs_3_), channel_id=1, source_target_pairs={{0,16},{16,0},{1,17},{17,1},{2,18},{18,2},{3,19},{19,3},{4,20},{20... | collective-permute-start | bytes 786440 | tf_op jit(solution)/shard_map/ppermute | solution.py:166
  83.7 2.7 %collective-permute-start.19 = (bf16[4,8,64,256]{3,2,1,0:T(8,128)(2,1)S(1)}, bf16[4,8,64,256]{3,2,1,0:T(8,128)(2,1)S(1)}, u32[]{:S(2)}, u32[]{:S(2)}) collective-permute-start(bf16[4,8,64,256]{3,2,1,0:T(8,128)(2,1)S(1)} %get-tuple-element.23), channel_id=1, source_target_pairs={{0,16},{16,0},{1,17},{17,1},{2,18},{18,2},{3,19},{19,3},{4,20},{20... | collective-permute-start | bytes 3145736 | tf_op jit(solution)/shard_map/ppermute | solution.py:166
  83.9 11.6 %collective-permute-start.15 = (bf16[4,8,64,256]{3,2,1,0:T(8,128)(2,1)S(1)}, bf16[4,8,64,256]{3,2,1,0:T(8,128)(2,1)S(1)}, u32[]{:S(2)}, u32[]{:S(2)}) collective-permute-start(bf16[4,8,64,256]{3,2,1,0:T(8,128)(2,1)S(1)} %get-tuple-element.18), channel_id=1, source_target_pairs={{0,16},{16,0},{1,17},{17,1},{2,18},{18,2},{3,19},{19,3},{4,20},{20... | collective-permute-start | bytes 3145736 | tf_op jit(solution)/shard_map/ppermute | solution.py:166
  93.4 12.2 %collective-permute-start.22 = (bf16[8,64,256]{2,1,0:T(8,128)(2,1)S(1)}, bf16[8,64,256]{2,1,0:T(8,128)(2,1)S(1)}, u32[]{:S(2)}, u32[]{:S(2)}) collective-permute-start(bf16[8,64,256]{2,1,0:T(8,128)(2,1)S(1)} %get-tuple-element.27), channel_id=1, source_target_pairs={{0,12},{4,0},{8,4},{12,8},{1,13},{5,1},{9,5},{13,9},{2,14},{6,2},{... | collective-permute-start | bytes 786440 | tf_op jit(solution)/shard_map/ppermute | solution.py:166
  93.5 12.9 %collective-permute-start.21 = (bf16[8,64,256]{2,1,0:T(8,128)(2,1)S(1)}, bf16[8,64,256]{2,1,0:T(8,128)(2,1)S(1)}, u32[]{:S(2)}, u32[]{:S(2)}) collective-permute-start(bf16[8,64,256]{2,1,0:T(8,128)(2,1)S(1)} %get-tuple-element.26), channel_id=1, source_target_pairs={{0,8},{4,12},{8,0},{12,4},{1,9},{5,13},{9,1},{13,5},{2,10},{6,14},... | collective-permute-start | bytes 786440 | tf_op jit(solution)/shard_map/ppermute | solution.py:166
  94.8 14.4 %collective-permute-start.20 = (bf16[8,64,256]{2,1,0:T(8,128)(2,1)S(1)}, bf16[8,64,256]{2,1,0:T(8,128)(2,1)S(1)}, u32[]{:S(2)}, u32[]{:S(2)}) collective-permute-start(bf16[8,64,256]{2,1,0:T(8,128)(2,1)S(1)} %get-tuple-element.25), channel_id=1, source_target_pairs={{0,4},{4,8},{8,12},{12,0},{1,5},{5,9},{9,13},{13,1},{2,6},{6,10},{... | collective-permute-start | bytes 786440 | tf_op jit(solution)/shard_map/ppermute | solution.py:166
  102.4 10.0 %collective-permute-start.18 = (bf16[8,64,256]{2,1,0:T(8,128)(2,1)S(1)}, bf16[8,64,256]{2,1,0:T(8,128)(2,1)S(1)}, u32[]{:S(2)}, u32[]{:S(2)}) collective-permute-start(bf16[8,64,256]{2,1,0:T(8,128)(2,1)S(1)} %get-tuple-element.22), channel_id=1, source_target_pairs={{0,12},{4,0},{8,4},{12,8},{1,13},{5,1},{9,5},{13,9},{2,14},{6,2},{... | collective-permute-start | bytes 786440 | tf_op jit(solution)/shard_map/ppermute | solution.py:166
  104.4 9.2 %collective-permute-start.17 = (bf16[8,64,256]{2,1,0:T(8,128)(2,1)S(1)}, bf16[8,64,256]{2,1,0:T(8,128)(2,1)S(1)}, u32[]{:S(2)}, u32[]{:S(2)}) collective-permute-start(bf16[8,64,256]{2,1,0:T(8,128)(2,1)S(1)} %get-tuple-element.21), channel_id=1, source_target_pairs={{0,8},{4,12},{8,0},{12,4},{1,9},{5,13},{9,1},{13,5},{2,10},{6,14},... | collective-permute-start | bytes 786440 | tf_op jit(solution)/shard_map/ppermute | solution.py:166
  105.6 14.6 %collective-permute-start.16 = (bf16[8,64,256]{2,1,0:T(8,128)(2,1)S(1)}, bf16[8,64,256]{2,1,0:T(8,128)(2,1)S(1)}, u32[]{:S(2)}, u32[]{:S(2)}) collective-permute-start(bf16[8,64,256]{2,1,0:T(8,128)(2,1)S(1)} %get-tuple-element.20), channel_id=1, source_target_pairs={{0,4},{4,8},{8,12},{12,0},{1,5},{5,9},{9,13},{13,1},{2,6},{6,10},{... | collective-permute-start | bytes 786440 | tf_op jit(solution)/shard_map/ppermute | solution.py:166
  109.3 10.9 %collective-permute-start.23 = (bf16[8,64,256]{2,1,0:T(8,128)(2,1)S(1)}, bf16[8,64,256]{2,1,0:T(8,128)(2,1)S(1)}, u32[]{:S(2)}, u32[]{:S(2)}) collective-permute-start(bf16[8,64,256]{2,1,0:T(8,128)(2,1)S(1)} %add_convert_fusion.1), channel_id=1, source_target_pairs={{0,2},{2,0},{1,3},{3,1},{4,6},{6,4},{5,7},{7,5},{8,10},{10,8},{9,1... | collective-permute-start | bytes 786440 | tf_op jit(solution)/shard_map/ppermute | solution.py:166
  (6 other events, 71.3 us)
